TPU v7x, 512 devices: a whole 4x4x16 slice. The times are simulated.
512 devices in a mesh: ctx: 128 (over x, z, core), head: 4 (over y).
Axes of the slice: x: 4, y: 4, z: 16, core: 2. Of those that a mesh axis runs over, the one named last changes fastest.
Arguments:
- queries: bfloat16 [4, 16384, 1024], P(None, 'ctx', 'head'), may hold values from -45 to 45
- keys: bfloat16 [4, 16384, 1024], P(None, 'ctx', 'head'), may hold values from -6 to 6
- values: bfloat16 [4, 16384, 1024], P(None, 'ctx', 'head'), may hold values from -6 to 6
- out_weight: bfloat16 [1024, 2048], P(None, 'head'), may hold values from -0.1875 to 0.1875
- global_ids: int32 [4, 2], replicated, may hold values from 0 to 255, as said below
- rand_ids: int32 [4, 256, 4], P(None, 'ctx'), may hold values from 0 to 255, as said below
- rand_count: int32 [4, 256], P(None, 'ctx'), may hold values from 1 to 4
Outputs:
- output: bfloat16 [4, 16384, 2048], P(None, 'ctx', 'head')
Inputs may be any that keep to these rules, and one draw needn't show every extreme that they name: `global_ids`: block ids; the 2 ids of one sequence are distinct. `rand_ids`: block ids of the same sequence. Taking together the 2 query blocks that each of the 4 sequences has on one index of ctx, at most 1 live slots name blocks held by any one index of ctx.
All inputs are finite; a program needn't handle non-finite values.
Results may differ from a plain program's by a relative error of at most 0.0056.
Values may be sent and summed in bfloat16 or wider, within the bound.
A program may use at most 64 MiB of HBM per device.

v0:
```python
import jax
import jax.numpy as jnp
from jax import lax
from jax.sharding import PartitionSpec as P

HEAD_DIM = 128
BLOCK = 64
GLOB = 2
RMAX = 4


def with_halo(cells, sides, width):
    for axis, dim in sides:
        count = lax.axis_size(axis)
        head = lax.slice_in_dim(cells, 0, width, axis=dim)
        tail = lax.slice_in_dim(cells, cells.shape[dim] - width, cells.shape[dim], axis=dim)
        cells = jnp.concatenate(
            [
                lax.ppermute(tail, axis, [(i, (i + 1) % count) for i in range(count)]),
                cells,
                lax.ppermute(head, axis, [((i + 1) % count, i) for i in range(count)]),
            ],
            axis=dim,
        )
    return cells


def slot_table(slot_of, live_flat, slot_total):
    return (
        (slot_of[:, None] == jnp.arange(slot_total, dtype=jnp.int32)[None, :]) & live_flat[:, None]
    ).astype(jnp.int32)


def on_device(queries, keys, values, out_weight, global_ids, rand_ids, rand_count):
    seq_count, seq_rows, local_width = queries.shape
    blocks_here = seq_rows // BLOCK
    heads_here = local_width // HEAD_DIM
    cycle_size = lax.axis_size("ctx")
    my_index = lax.axis_index("ctx")
    request_count = seq_count * blocks_here * RMAX
    capacity = (request_count + cycle_size - 1) // cycle_size
    slot_total = cycle_size * capacity
    key_width = 3 + GLOB + RMAX
    score_scale = HEAD_DIM ** (-0.5)
    token_pairs = jnp.stack([keys, values], 0)
    block_pairs = jnp.stack(
        [
            keys.reshape(seq_count, blocks_here, BLOCK, local_width),
            values.reshape(seq_count, blocks_here, BLOCK, local_width),
        ],
        2,
    ).reshape(seq_count * blocks_here, 2, BLOCK, local_width)
    extended = with_halo(token_pairs, (("ctx", 2),), BLOCK)
    own_blocks = token_pairs.reshape(2, seq_count, blocks_here, BLOCK, local_width)
    shared_owner = global_ids // blocks_here
    shared_local = global_ids % blocks_here
    picker = (
        (shared_local[:, :, None] == jnp.arange(blocks_here, dtype=jnp.int32)[None, None, :])
        & (shared_owner == my_index)[:, :, None]
    ).astype(jnp.bfloat16)
    contribution = jnp.einsum(
        "sgj,xsjtf->xsgtf", picker, own_blocks, preferred_element_type=jnp.float32
    )
    shared_rows = lax.psum(contribution, "ctx").astype(jnp.bfloat16)
    slot_ids = jnp.arange(RMAX, dtype=jnp.int32)
    live_flat = (slot_ids[None, None, :] < rand_count[:, :, None]).reshape(-1)
    owners = (rand_ids // blocks_here).reshape(-1)
    seq_of = jnp.arange(seq_count, dtype=jnp.int32)[:, None, None]
    block_codes = (seq_of * blocks_here + rand_ids % blocks_here).reshape(-1)
    hit_owner = (
        (owners[:, None] == jnp.arange(cycle_size, dtype=jnp.int32)[None, :]) & live_flat[:, None]
    ).astype(jnp.int32)
    rank_within = jnp.sum((jnp.cumsum(hit_owner, axis=0) - hit_owner) * hit_owner, axis=1)
    slot_of = jnp.where(live_flat, owners * capacity + rank_within, 0)
    slot_hits = slot_table(slot_of, live_flat, slot_total)
    requests_out = (jnp.sum(slot_hits * (block_codes[:, None] + 1), axis=0) - 1).reshape(
        cycle_size, capacity
    )
    wanted_here = lax.all_to_all(requests_out, "ctx", split_axis=0, concat_axis=0, tiled=True)
    beside_all = extended.reshape(2, seq_count, blocks_here + 2, BLOCK, local_width)
    window_keys = jnp.stack(
        [beside_all[:, :, offset : offset + blocks_here] for offset in range(3)], 3
    )
    shared_wide = jnp.broadcast_to(
        shared_rows[:, :, None], (2, seq_count, blocks_here, GLOB, BLOCK, local_width)
    )
    local_keys = jnp.concatenate([window_keys, shared_wide], 3)
    query_view = queries.reshape(seq_count, blocks_here, BLOCK, heads_here, HEAD_DIM)
    payload = jnp.take(block_pairs, jnp.maximum(wanted_here, 0).reshape(-1), axis=0).reshape(
        cycle_size, capacity, 2, BLOCK, local_width
    )
    received = lax.all_to_all(payload, "ctx", split_axis=0, concat_axis=0, tiled=True)
    random_rows = jnp.take(received.reshape(slot_total, 2, BLOCK, local_width), slot_of, axis=0)
    random_rows = jnp.moveaxis(
        random_rows.reshape(seq_count, blocks_here, RMAX, 2, BLOCK, local_width), 3, 0
    )
    all_keys = jnp.concatenate([local_keys, random_rows], 3).reshape(
        2, seq_count, blocks_here, key_width * BLOCK, heads_here, HEAD_DIM
    )
    scores = (
        jnp.einsum(
            "sjqhd,sjkhd->sjhqk", query_view, all_keys[0], preferred_element_type=jnp.float32
        )
        * score_scale
    )
    live_slots = jnp.concatenate(
        [
            jnp.ones((seq_count, blocks_here, 3 + GLOB), jnp.bool_),
            slot_ids[None, None, :] < rand_count[:, :, None],
        ],
        2,
    )
    live_cols = jnp.repeat(live_slots, BLOCK, axis=2)[:, :, None, None, :]
    masked = jnp.where(live_cols, scores, -1e30)
    row_peak = jnp.max(masked, axis=-1, keepdims=True)
    weights = jnp.where(live_cols, jnp.exp(masked - row_peak), 0.0)
    row_total = jnp.sum(weights, axis=-1)
    weighted = jnp.einsum(
        "sjhqk,sjkhd->sjqhd",
        weights.astype(jnp.bfloat16),
        all_keys[1],
        preferred_element_type=jnp.float32,
    )
    attention = (
        (weighted / jnp.moveaxis(row_total, 2, 3)[..., None])
        .astype(jnp.bfloat16)
        .reshape(seq_count, seq_rows, local_width)
    )
    projected = jnp.einsum(
        "stf,fo->sto",
        lax.all_gather(attention, "head", axis=2, tiled=True),
        out_weight,
        preferred_element_type=jnp.float32,
    )
    return projected.astype(jnp.bfloat16)


def solution(mesh):
    placed = (
        P(None, "ctx", "head"),
        P(None, "ctx", "head"),
        P(None, "ctx", "head"),
        P(None, "head"),
        P(),
        P(None, "ctx", None),
        P(None, "ctx"),
    )
    return jax.shard_map(
        on_device, mesh=mesh, in_specs=placed, out_specs=P(None, "ctx", "head"), check_vma=False
    )
```

profile of v0, /device:TPU:2, one launch (start us, length us, event | category | flops | bytes accessed | tf_op | source)
XLA Modules:
  0.0 992.5 jit_solution(1690685669492652247)
XLA Ops:
  6.5 0.0 copy-start
  6.5 0.9 copy.54
  7.4 0.1 iota_compare_fusion.2
  7.5 0.1 lt.84
  7.6 0.8 and_select_fusion.1
  8.3 0.1 reshape.187
  8.4 0.1 fusion.37
  8.5 0.1 reduce_window_sum.11
  8.5 0.2 select_reduce_fusion.1
  8.7 0.1 add.104
  8.8 0.1 select_reduce_fusion
  8.9 0.7 copy.55
  9.7 19.5 %all-to-all-start = ((s32[128,1,1]{2,1,0:T(1,128)}), s32[128,1,1]{2,1,0:T(1,128)S(1)}, u32[]{:S(2)}, u32[]{:S(2)}) async-start(s32[128,1,1]{2,1,0:T(1,128)} %copy.55), calls=%async_computation | async-start | bytes 131072 | tf_op jit(solution)/shard_map/all_to_all | solution.py:79
  29.2 1.1 pad_maximum_fusion.3
  30.3 13.3 %all-to-all-done = s32[128,1,1]{2,1,0:T(1,128)S(1)} async-done(((s32[128,1,1]{2,1,0:T(1,128)}), s32[128,1,1]{2,1,0:T(1,128)S(1)}, u32[]{:S(2)}, u32[]{:S(2)}) %all-to-all-start) | async-done | bytes 544 | tf_op jit(solution)/shard_map/all_to_all | solution.py:79
  43.6 2.4 maximum_reduce_fusion
  46.0 6.3 gather_fusion
  52.3 2.4 compare_reduce_fusion
  54.6 7.4 bitcast_select_fusion
  62.1 8.6 all-to-all-start.1
  70.7 0.0 all-gather.2.cloned.1.call-start
  70.7 0.0 copy-done.1
  70.8 0.0 copy-done.2
  70.8 2.1 collective-permute-start
  72.9 5.6 collective-permute-start.1
  78.5 0.1 reshape.189
  78.6 0.1 lt.87
  78.7 0.3 copy.49
  79.0 0.3 copy.50
  79.3 0.1 copy.51
  79.4 0.1 copy.52
  79.5 1.8 convolution_bitcast_fusion
  81.2 774.6 %all-reduce.2 = bf16[2,4,2,64,256]{4,2,3,0,1:T(2,128)(2,1)S(1)} all-reduce(f32[2,4,2,64,256]{4,2,3,0,1:T(2,128)} %convolution_bitcast_fusion), channel_id=1, replica_groups=mesh['ctx'=128,'head'=4] {'ctx'}, use_global_device_ids=true, to_apply=%region_0.1 | all-reduce | flops 262144 | bytes 1572864 | tf_op jit(solution)/shard_map/psum | solution.py:64
  855.8 0.1 reduce_sum.32
  855.9 0.1 copy.53
  856.0 0.0 copy-done.4
  856.0 0.8 reshape.190
  856.8 0.1 concatenate.13.clone
  856.9 0.1 broadcast_in_dim.78
  857.0 0.1 broadcast_in_dim.79
  857.1 0.1 compare_and_fusion
  857.2 0.0 collective-permute-done
  857.2 0.0 collective-permute-done.1
  857.2 1.1 pad_maximum_fusion
  858.3 0.8 fusion.32
  859.1 0.8 fusion.31
  859.9 0.8 fusion.30
  860.8 1.1 broadcast_dynamic-update-slice_fusion
  861.9 0.0 all-to-all-done.1
  861.9 4.1 gather_fusion.1
  866.0 2.3 bitcast_dynamic-update-slice_fusion
  868.3 5.2 fusion.51
  873.5 4.6 squeeze.7
  878.1 5.7 squeeze.6
  883.9 1.9 fusion.6
  885.7 0.0 copy-start.3
  885.8 1.2 fusion.52
  886.9 0.5 copy-done.3
  887.4 0.6 fusion.24
  888.0 0.3 copy.65
  888.3 0.9 reshape.191
  889.2 0.0 all-gather.2.cloned.1.call-update
  889.2 93.7 %all-gather.2.cloned.1.call-done = bf16[4,128,1024]{2,1,0:T(8,128)(2,1)} async-done(((bf16[4,128,256]{2,1,0:T(8,128)(2,1)}), bf16[4,128,1024]{2,1,0:T(8,128)(2,1)}) %all-gather.2.cloned.1.call-update) | async-done | bytes 1048592 | tf_op jit(solution)/shard_map/all_gather | solution.py:131
  982.9 2.7 convolution_convert_fusion
  (17 shorter events, 0.1 us)
Async XLA Ops:
  6.5 976.4 %copy-start = (bf16[1024,512]{1,0:T(8,128)(2,1)S(1)}, bf16[1024,512]{1,0:T(8,128)(2,1)}, u32[]{:S(2)}) copy-start(bf16[1024,512]{1,0:T(8,128)(2,1)} %param.10) | copy-start | bytes 3145732
  9.7 33.9 %all-to-all-start = ((s32[128,1,1]{2,1,0:T(1,128)}), s32[128,1,1]{2,1,0:T(1,128)S(1)}, u32[]{:S(2)}, u32[]{:S(2)}) async-start(s32[128,1,1]{2,1,0:T(1,128)} %copy.55), calls=%async_computation | async-start | bytes 131072 | tf_op jit(solution)/shard_map/all_to_all | solution.py:79
  62.0 8.7 copy-start.1
  62.0 8.7 copy-start.2
  62.1 17.2 %copy-start.5 = (s32[4,2]{0,1:T(2,128)S(1)}, s32[4,2]{0,1:T(2,128)}, u32[]{:S(2)}) copy-start(s32[4,2]{0,1:T(2,128)} %param.11) | copy-start | bytes 100
  62.1 799.9 %all-to-all-start.1 = ((bf16[128,1,2,64,256]{4,3,2,1,0:T(8,128)(2,1)}), bf16[128,1,2,64,256]{4,3,2,1,0:T(8,128)(2,1)}, u32[]{:S(2)}, u32[]{:S(2)}) async-start(bf16[128,1,2,64,256]{4,3,2,1,0:T(8,128)(2,1)} %bitcast_select_fusion), calls=%async_computation.1 | async-start | bytes 16777216 | tf_op jit(solution)/shard_map/all_to_all | solution.py:92
  70.7 912.2 %all-gather.2.cloned.1.call-start = ((), (), s32[]{:S(2)}) async-start(), calls=%async_computation.2 | async-start | bytes 1310720 | tf_op jit(solution)/shard_map/all_gather | solution.py:131
  70.8 786.3 %collective-permute-start = (bf16[2,4,64,256]{3,2,1,0:T(8,128)(2,1)S(1)}, bf16[2,4,64,256]{3,2,1,0:T(8,128)(2,1)}, u32[]{:S(2)}, u32[]{:S(2)}) collective-permute-start(bf16[2,4,64,256]{3,2,1,0:T(8,128)(2,1)S(1)} %get-tuple-element.7), channel_id=1, source_target_pairs={{0,4},{4,8},{8,12},{12,16},{16,20},{20,24},{24,28},{28,32},{32,36}... | collective-permute-start | bytes 786440 | tf_op jit(solution)/shard_map/ppermute | solution.py:19
  72.9 784.3 %collective-permute-start.1 = (bf16[2,4,64,256]{3,2,1,0:T(8,128)(2,1)S(1)}, bf16[2,4,64,256]{3,2,1,0:T(8,128)(2,1)}, u32[]{:S(2)}, u32[]{:S(2)}) collective-permute-start(bf16[2,4,64,256]{3,2,1,0:T(8,128)(2,1)S(1)} %get-tuple-element.8), channel_id=1, source_target_pairs={{4,0},{8,4},{12,8},{16,12},{20,16},{24,20},{28,24},{32,28},{36,32}... | collective-permute-start | bytes 786440 | tf_op jit(solution)/shard_map/ppermute | solution.py:21
  79.5 776.5 %copy-start.4 = (bf16[4,128,256]{2,1,0:T(8,128)(2,1)S(1)}, bf16[4,128,256]{2,1,0:T(8,128)(2,1)}, u32[]{:S(2)}) copy-start(bf16[4,128,256]{2,1,0:T(8,128)(2,1)} %param.7) | copy-start | bytes 786436
  885.7 1.7 copy-start.3
Sparse Core Ops, SparseCore 0:
  889.3 93.5 all-gather.1
where the time goes:
time: 993 us; the launch traced here: 992 us
  blocking collectives  775 us (78%)
  waiting for transfers between devices  107 us (11%)
  starting transfers between devices  35.9 us (4%)
  local copies, waits for them, and re-layouts  35.2 us (4%)
  other arithmetic  19.2 us (2%)
  between operations  13.6 us (1%)
    psum x1, blocking collectives, on_device(): shared_rows = lax.psum(contribution, 'ctx').astype(jnp.bfloat16)  775 us
    all_gather x1, waiting for transfers between devices, on_device(): lax.all_gather(attention, 'head', axis=2, tiled=True)  93.7 us
  transfers between devices with their start and end apart: 5, of which 2 were waited for; matrix products, arithmetic and copies ran while one was open for 1% of the time, Pallas kernels for 0%

commit v1 on v0

--- a/solution.py
+++ b/solution.py
@@ -7,6 +7,22 @@
 BLOCK = 64
 GLOB = 2
 RMAX = 4
+
+
+def product_in_turn(shard, axis, dim, term):
+    peers, position, span = (lax.axis_size(axis), lax.axis_index(axis), shard.shape[dim])
+    right = [(i, (i + 1) % peers) for i in range(peers)]
+    downward = [(i, (i - 1) % peers) for i in range(peers)]
+    halfway = peers // 2
+    from_left = from_right = shard
+    total = term(shard, position * span)
+    for step in range(1, halfway + 1):
+        from_left = lax.ppermute(from_left, axis, right)
+        if step < peers - halfway:
+            from_right = lax.ppermute(from_right, axis, downward)
+            total = total + term(from_right, (position + step) % peers * span)
+        total = total + term(from_left, (position - step) % peers * span)
+    return total
 
 
 def with_halo(cells, sides, width):
@@ -126,11 +142,16 @@
         .astype(jnp.bfloat16)
         .reshape(seq_count, seq_rows, local_width)
     )
-    projected = jnp.einsum(
-        "stf,fo->sto",
-        lax.all_gather(attention, "head", axis=2, tiled=True),
-        out_weight,
-        preferred_element_type=jnp.float32,
+    projected = product_in_turn(
+        attention,
+        "head",
+        2,
+        lambda own_block, at: jnp.einsum(
+            "stf,fo->sto",
+            own_block,
+            lax.dynamic_slice_in_dim(out_weight, at, own_block.shape[2], axis=0),
+            preferred_element_type=jnp.float32,
+        ),
     )
     return projected.astype(jnp.bfloat16)
 

time: 993 us -> 973 us (0.980)
  the two profiles are of different devices: /device:TPU:2 before, /device:TPU:16 now
where the time goes in v1:
time: 973 us
  blocking collectives  844 us (87%)
  starting transfers between devices  45.3 us (5%)
  local copies, waits for them, and re-layouts  34.5 us (4%)
  waiting for transfers between devices  22.7 us (2%)
  other arithmetic  19.2 us (2%)
    psum x1, blocking collectives, on_device(): shared_rows = lax.psum(contribution, 'ctx').astype(jnp.bfloat16)  844 us
    all_to_all x1, starting transfers between devices, on_device(): lax.all_to_all(requests_out, 'ctx', split_axis=0, concat_axis=0, tiled=True)  19.8 us
  transfers between devices with their start and end apart: 7, of which 3 were waited for; matrix products, arithmetic and copies ran while one was open for 1% of the time, Pallas kernels for 0%

profile of v1, /device:TPU:16, one launch (start us, length us, event | category | flops | bytes accessed | tf_op | source)
XLA Modules:
  0.0 972.6 jit_solution(10919166663085651145)
XLA Ops:
  0.0 0.9 copy.54
  0.9 0.1 iota_compare_fusion.2
  0.9 0.1 lt.110
  1.0 0.8 and_select_fusion.1
  1.8 0.1 reshape.187
  1.9 0.1 fusion.46
  2.0 0.1 reduce_window_sum.11
  2.0 0.2 select_reduce_fusion.1
  2.2 0.1 add.140
  2.3 0.1 select_reduce_fusion
  2.4 0.7 copy.55
  3.2 19.8 %all-to-all-start = ((s32[128,1,1]{2,1,0:T(1,128)}), s32[128,1,1]{2,1,0:T(1,128)S(1)}, u32[]{:S(2)}, u32[]{:S(2)}) async-start(s32[128,1,1]{2,1,0:T(1,128)} %copy.55), calls=%async_computation | async-start | bytes 131072 | tf_op jit(solution)/shard_map/all_to_all | solution.py:95
  22.9 1.1 pad_maximum_fusion.3
  24.0 14.4 %all-to-all-done = s32[128,1,1]{2,1,0:T(1,128)S(1)} async-done(((s32[128,1,1]{2,1,0:T(1,128)}), s32[128,1,1]{2,1,0:T(1,128)S(1)}, u32[]{:S(2)}, u32[]{:S(2)}) %all-to-all-start) | async-done | bytes 544 | tf_op jit(solution)/shard_map/all_to_all | solution.py:95
  38.4 2.4 maximum_reduce_fusion
  40.8 6.3 gather_fusion
  47.1 2.4 compare_reduce_fusion
  49.4 7.4 bitcast_select_fusion
  56.9 7.6 all-to-all-start.1
  64.6 1.9 collective-permute-start
  66.5 7.0 collective-permute-start.1
  73.5 0.1 reshape.189
  73.5 0.1 lt.113
  73.7 0.1 copy.52
  73.8 0.3 copy.49
  74.0 0.3 copy.50
  74.3 0.1 copy.51
  74.4 1.8 convolution_bitcast_fusion
  76.2 844.4 %all-reduce.2 = bf16[2,4,2,64,256]{4,2,3,0,1:T(2,128)(2,1)S(1)} all-reduce(f32[2,4,2,64,256]{4,2,3,0,1:T(2,128)} %convolution_bitcast_fusion), channel_id=1, replica_groups=mesh['ctx'=128,'head'=4] {'ctx'}, use_global_device_ids=true, to_apply=%region_0.1 | all-reduce | flops 262144 | bytes 1572864 | tf_op jit(solution)/shard_map/psum | solution.py:80
  920.6 0.1 reduce_sum.32
  920.7 0.1 copy.53
  920.8 0.8 reshape.190
  921.5 0.1 concatenate.13.clone
  921.6 0.1 broadcast_in_dim.78
  921.7 0.1 broadcast_in_dim.79
  921.8 0.1 compare_and_fusion
  921.9 0.0 collective-permute-done
  921.9 0.0 collective-permute-done.1
  921.9 1.1 pad_maximum_fusion
  923.0 0.8 fusion.32
  923.9 0.8 fusion.31
  924.7 0.8 fusion.30
  925.5 1.1 broadcast_dynamic-update-slice_fusion
  926.6 0.0 all-to-all-done.1
  926.6 4.1 gather_fusion.1
  930.7 2.3 bitcast_dynamic-update-slice_fusion
  933.0 5.2 fusion.64
  938.3 4.6 squeeze.7
  942.9 5.7 squeeze.6
  948.6 1.9 fusion.6
  950.5 1.2 fusion.65
  951.7 0.5 copy-done.3
  952.2 0.6 fusion.25
  952.8 0.3 copy.65
  953.0 0.2 reshape.191
  953.2 3.2 collective-permute-start.3
  956.4 2.7 collective-permute-start.2
  959.1 0.3 fusion.38
  959.4 3.9 collective-permute-done.3
  963.3 3.2 collective-permute-start.4
  966.5 0.3 convolution_add_fusion.2
  966.8 0.3 convolution_add_fusion.1
  967.1 4.4 collective-permute-done.4
  971.6 1.1 fusion.14
  (23 shorter events, 0.1 us)
Async XLA Ops:
  0.0 959.1 %copy-start = (bf16[1024,512]{1,0:T(8,128)(2,1)S(1)}, bf16[1024,512]{1,0:T(8,128)(2,1)}, u32[]{:S(2)}) copy-start(bf16[1024,512]{1,0:T(8,128)(2,1)} %param.10) | copy-start | bytes 3145732
  3.2 35.3 %all-to-all-start = ((s32[128,1,1]{2,1,0:T(1,128)}), s32[128,1,1]{2,1,0:T(1,128)S(1)}, u32[]{:S(2)}, u32[]{:S(2)}) async-start(s32[128,1,1]{2,1,0:T(1,128)} %copy.55), calls=%async_computation | async-start | bytes 131072 | tf_op jit(solution)/shard_map/all_to_all | solution.py:95
  56.9 7.6 copy-start.1
  56.9 7.6 copy-start.2
  56.9 16.8 %copy-start.5 = (s32[4,2]{0,1:T(2,128)S(1)}, s32[4,2]{0,1:T(2,128)}, u32[]{:S(2)}) copy-start(s32[4,2]{0,1:T(2,128)} %param.11) | copy-start | bytes 100
  56.9 869.8 %all-to-all-start.1 = ((bf16[128,1,2,64,256]{4,3,2,1,0:T(8,128)(2,1)}), bf16[128,1,2,64,256]{4,3,2,1,0:T(8,128)(2,1)}, u32[]{:S(2)}, u32[]{:S(2)}) async-start(bf16[128,1,2,64,256]{4,3,2,1,0:T(8,128)(2,1)} %bitcast_select_fusion), calls=%async_computation.1 | async-start | bytes 16777216 | tf_op jit(solution)/shard_map/all_to_all | solution.py:108
  64.6 857.3 %collective-permute-start = (bf16[2,4,64,256]{3,2,1,0:T(8,128)(2,1)S(1)}, bf16[2,4,64,256]{3,2,1,0:T(8,128)(2,1)}, u32[]{:S(2)}, u32[]{:S(2)}) collective-permute-start(bf16[2,4,64,256]{3,2,1,0:T(8,128)(2,1)S(1)} %get-tuple-element.7), channel_id=1, source_target_pairs={{0,4},{4,8},{8,12},{12,16},{16,20},{20,24},{24,28},{28,32},{32,36}... | collective-permute-start | bytes 786440 | tf_op jit(solution)/shard_map/ppermute | solution.py:35
  66.5 855.4 %collective-permute-start.1 = (bf16[2,4,64,256]{3,2,1,0:T(8,128)(2,1)S(1)}, bf16[2,4,64,256]{3,2,1,0:T(8,128)(2,1)}, u32[]{:S(2)}, u32[]{:S(2)}) collective-permute-start(bf16[2,4,64,256]{3,2,1,0:T(8,128)(2,1)S(1)} %get-tuple-element.8), channel_id=1, source_target_pairs={{4,0},{8,4},{12,8},{16,12},{20,16},{24,20},{28,24},{32,28},{36,32}... | collective-permute-start | bytes 786440 | tf_op jit(solution)/shard_map/ppermute | solution.py:37
  74.4 846.3 %copy-start.4 = (bf16[4,128,256]{2,1,0:T(8,128)(2,1)S(1)}, bf16[4,128,256]{2,1,0:T(8,128)(2,1)}, u32[]{:S(2)}) copy-start(bf16[4,128,256]{2,1,0:T(8,128)(2,1)} %param.7) | copy-start | bytes 786436
  950.5 1.7 copy-start.3
  953.2 10.1 %collective-permute-start.3 = (bf16[4,128,256]{2,1,0:T(8,128)(2,1)S(1)}, bf16[4,128,256]{2,1,0:T(8,128)(2,1)S(1)}, u32[]{:S(2)}, u32[]{:S(2)}) collective-permute-start(bf16[4,128,256]{2,1,0:T(8,128)(2,1)S(1)} %reshape.191), channel_id=1, source_target_pairs={{0,1},{1,2},{2,3},{3,0},{4,5},{5,6},{6,7},{7,4},{8,9},{9,10},{10,1... | collective-permute-start | bytes 786440 | tf_op jit(solution)/shard_map/ppermute | solution.py:20
  956.4 10.1 %collective-permute-start.2 = (bf16[4,128,256]{2,1,0:T(8,128)(2,1)S(1)}, bf16[4,128,256]{2,1,0:T(8,128)(2,1)S(1)}, u32[]{:S(2)}, u32[]{:S(2)}) collective-permute-start(bf16[4,128,256]{2,1,0:T(8,128)(2,1)S(1)} %reshape.191), channel_id=1, source_target_pairs={{0,3},{1,0},{2,1},{3,2},{4,7},{5,4},{6,5},{7,6},{8,11},{9,8},{10,9... | collective-permute-start | bytes 786440 | tf_op jit(solution)/shard_map/ppermute | solution.py:22
  963.3 8.3 collective-permute-start.4
